TPU v7x, 512 devices: a whole 4x8x8 slice. The times are simulated.
512 devices in a mesh: sect: 4 (over z_lo, core), blk: 128 (over z_hi, x, y).
Axes of the slice: x: 4, y: 8, z: 8 (z_hi: 4, z_lo: 2; z = z_hi * 2 + z_lo), core: 2. Of those that a mesh axis runs over, the one named last changes fastest.
Arguments:
- last_perceptron_activations: bfloat16 [512, 192, 4304], P(('sect', 'blk')), may hold values from -6 to 6
- caption_reduction_matrix: bfloat16 [4304, 1152], P(None, 'blk'), may hold values from -0.09375 to 0.09375
- picture_reduction_matrix: bfloat16 [4304, 1152], P(None, 'blk'), may hold values from -0.09375 to 0.09375
- caption_offset_vector: float32 [1152], replicated, may hold values from -0.6 to 0.6
- picture_offset_vector: float32 [1152], replicated, may hold values from -0.6 to 0.6
- score_multiplier_array: float32 [1], replicated, may hold values from 4 to 16
- match_score_offset: float32 [1], replicated, may hold values from -6 to -2
- caption_match_position: int32 [384], replicated, may hold values from 0 to 383, each once
Outputs:
- text_grad: float32 [384, 4304], P('blk', 'sect')
Inputs may be any that keep to these rules, and one draw needn't show every extreme that they name: `caption_match_position`: each text index appears exactly once, so every image has exactly one paired text.
All inputs are finite; a program needn't handle non-finite values.
Results may differ from a plain program's by a relative error of at most 0.013.
Values may be sent and summed in bfloat16 or wider, within the bound.
A program may use at most 128 MiB of HBM per device.

v0:
```python
import jax
import jax.numpy as jnp
from jax import lax
from jax.sharding import Mesh
from jax.sharding import PartitionSpec as P

D = 1152
FF = 4304
TXT_LEN = 64
IMG_TOK = 192
BLK = ("blk_0", "blk_1", "blk_2")
SECT_BLK = ("sect", "blk_0", "blk_1", "blk_2")


def broadcast(x, axis, root):
    return lax.dynamic_index_in_dim(lax.all_gather(x, axis), root, 0, keepdims=False)


def joined_along(parts, dim):
    lengths = list(parts.shape[1:])
    lengths[dim] *= parts.shape[0]
    return jnp.moveaxis(parts, 0, dim).reshape(lengths)


def gather_in_order(x, axes, sequence):
    parts = x[None]
    for k in sequence:
        parts = lax.all_gather(parts, axes[k], axis=0, tiled=True)
    held = [lax.axis_size(axes[k]) for k in reversed(sequence)]
    parts = parts.reshape(*held, *x.shape)
    turned = sorted(range(len(sequence)), key=lambda place: sequence[len(sequence) - 1 - place])
    return parts.transpose(*turned, *range(len(sequence), parts.ndim)).reshape(-1, *x.shape)


def gathered_by_axis(x, axes, sequence, dim):
    return joined_along(gather_in_order(x, axes, sequence), dim)


def reduced_to_own(parts, axes, sequence):
    inside = parts.shape[1:]
    parts = parts.reshape(*(lax.axis_size(a) for a in axes), *inside)
    parts = jnp.moveaxis(parts, sequence, range(len(axes))).reshape(-1, *inside)
    for k in sequence:
        parts = lax.psum_scatter(parts, axes[k], scatter_dimension=0, tiled=True)
    return parts[0]


def cut_along(x, dim, count):
    before, after = (x.shape[:dim], x.shape[dim + 1 :])
    return jnp.moveaxis(x.reshape(*before, count, -1, *after), dim, 0)


def summed_rows(x, axes, sequence, dim):
    count = lax.axis_size(axes)
    return reduced_to_own(cut_along(x, dim, count), axes, sequence)


def copy_for_each(x, axis):
    count = lax.axis_size(axis)
    return lax.all_to_all(jnp.broadcast_to(x[None], (count, *x.shape)), axis, 0, 0, tiled=True)


def of_everyone(x, axis):
    return copy_for_each(x, axis).sum(axis=0)


def unit_rows(pool):
    inv = lax.rsqrt(jnp.sum(pool * pool, axis=-1, keepdims=True) + 1e-06)
    return (pool * inv, inv)


def on_device(
    last_perceptron_activations,
    caption_reduction_matrix,
    picture_reduction_matrix,
    caption_offset_vector,
    picture_offset_vector,
    score_multiplier_array,
    match_score_offset,
    caption_match_position,
):
    hidden = last_perceptron_activations[0]
    sect_index = lax.axis_index("sect")
    blk_index = lax.axis_index(BLK)
    blk_count = lax.axis_size(BLK)
    sect_count = lax.axis_size("sect")
    rows = hidden.shape[0]
    txt_count = rows // TXT_LEN
    img_count = rows // IMG_TOK
    width = FF // sect_count
    is_text = sect_index == 0
    live = jnp.where(is_text, 0.0, 1.0).astype(jnp.float32)
    w_local = jnp.where(is_text, caption_reduction_matrix, picture_reduction_matrix)
    outs = jnp.dot(
        hidden, lax.all_gather(w_local, BLK, axis=1, tiled=True), preferred_element_type=jnp.float32
    )
    text_pool = jnp.mean(outs.reshape(txt_count, TXT_LEN, D), axis=1) + caption_offset_vector
    image_pool = jnp.mean(outs.reshape(img_count, IMG_TOK, D), axis=1) + picture_offset_vector
    text_pool = broadcast(text_pool, "sect", 0)
    text_unit, text_inv = unit_rows(text_pool)
    image_unit, image_inv = unit_rows(image_pool)
    text_emb = text_unit.astype(jnp.bfloat16)
    image_emb = image_unit.astype(jnp.bfloat16)
    similarity_multiplier = score_multiplier_array[0]
    shift_bias = match_score_offset[0]
    first = jnp.maximum((sect_index - 1) * blk_count + blk_index, 0) * img_count
    mine = lax.dynamic_slice_in_dim(caption_match_position, first, img_count)
    all_texts = gathered_by_axis(text_emb, BLK, (0, 1, 2), 0)
    count = all_texts.shape[0]
    logits = (
        similarity_multiplier
        * lax.dot_general(
            image_emb, all_texts, (((1,), (1,)), ((), ())), preferred_element_type=jnp.float32
        )
        + shift_bias
    )
    index_row = jnp.arange(count, dtype=jnp.int32)
    label = jnp.where(mine[:, None] == index_row[None, :], 1.0, -1.0).astype(jnp.float32)
    coef = (-label * jax.nn.sigmoid(-label * logits) * live).astype(jnp.bfloat16)
    acc_full = lax.dot_general(
        coef, image_emb, (((0,), (0,)), ((), ())), preferred_element_type=jnp.float32
    )
    acc = summed_rows(acc_full, BLK, (1, 2, 0), 0)
    acc = of_everyone(acc, "sect")
    grad = similarity_multiplier * acc
    grad_pool = (grad - text_unit * jnp.sum(text_unit * grad, axis=-1, keepdims=True)) * text_inv
    dy = grad_pool.astype(jnp.bfloat16)
    w_rows = lax.dynamic_slice_in_dim(caption_reduction_matrix, sect_index * width, width, 0)
    return lax.dot_general(
        dy,
        gathered_by_axis(w_rows, BLK, (0, 1, 2), 1),
        (((1,), (1,)), ((), ())),
        preferred_element_type=jnp.float32,
    )


def solution(mesh):
    finer = Mesh(
        mesh.devices.reshape(mesh.shape["sect"], 4, 4, 8), ("sect", "blk_0", "blk_1", "blk_2")
    )
    placed = (P(SECT_BLK, None, None), P(None, BLK), P(None, BLK), P(), P(), P(), P(), P())
    return jax.shard_map(
        on_device, mesh=finer, in_specs=placed, out_specs=P(BLK, "sect"), check_vma=False
    )
```

profile of v0, /device:TPU:2, one launch (start us, length us, event | category | flops | bytes accessed | tf_op | source)
XLA Modules:
  0.0 512.0 jit_solution(2313802400999751418)
XLA Ops:
  6.5 1.7 select_bitcast_fusion
  9.6 1.3 dynamic_slice.10
  10.9 225.3 %all-gather.8.cloned.1.call-done = bf16[128,9,4304]{2,1,0:T(8,128)(2,1)} async-done(((bf16[1,9,4304]{2,1,0:T(8,128)(2,1)}), bf16[128,9,4304]{2,1,0:T(8,128)(2,1)}) %all-gather.8.cloned.1.call-update) | async-done | bytes 9916432 | tf_op jit(solution)/shard_map/all_gather | solution.py:95
  236.2 17.9 %reshape.152 = bf16[1152,4304]{1,0:T(8,128)(2,1)} reshape(bf16[128,9,4304]{2,1,0:T(8,128)(2,1)} %all-gather.8.cloned.1.call-done) | data formatting | bytes 19832832
  254.1 7.3 %fusion.14 = (f32[1152]{0:T(1024)S(1)}, f32[1152,192]{0,1:T(8,128)S(1)}) fusion(bf16[1152,4304]{1,0:T(8,128)(2,1)} %reshape.152, bf16[1,192,4304]{2,1,0:T(8,128)(2,1)S(1)} %copy-done), kind=kOutput, calls=%fused_computation.32 | convolution fusion | flops 1904171904 | bytes 12458496 | tf_op jit(solution)/shard_map/dot_general | solution.py:94
  261.5 5.3 %all_gather.26 = f32[4,3,1152]{2,1,0:T(4,128)S(1)} all-gather(f32[1,3,1152]{2,1,0:T(4,128)S(1)} %bitcast_add_fusion), channel_id=1, replica_groups=mesh['sect'=4,'blk_0'=4,'blk_1'=4,'blk_2'=8] {'sect'}, dimensions={0}, use_global_device_ids=true | all-gather | bytes 69120 | tf_op jit(solution)/shard_map/all_gather | solution.py:16
  266.9 13.7 %all_gather.27 = bf16[4,3,1152]{2,1,0:T(4,128)(2,1)S(1)} all-gather(bf16[1,3,1152]{2,1,0:T(4,128)(2,1)S(1)} %multiply_convert_fusion), channel_id=1, replica_groups=mesh['sect'=4,'blk_0'=4,'blk_1'=4,'blk_2'=8] {'blk_0'}, dimensions={0}, use_global_device_ids=true | all-gather | bytes 34560 | tf_op jit(solution)/shard_map/all_gather | solution.py:28
  280.7 12.1 %all_gather.28 = bf16[16,3,1152]{2,1,0:T(4,128)(2,1)S(1)} all-gather(bf16[4,3,1152]{2,1,0:T(4,128)(2,1)S(1)} %all_gather.27), channel_id=1, replica_groups=mesh['sect'=4,'blk_0'=4,'blk_1'=4,'blk_2'=8] {'blk_1'}, dimensions={0}, use_global_device_ids=true | all-gather | bytes 138240 | tf_op jit(solution)/shard_map/all_gather | solution.py:28
  292.8 26.3 %all_gather.29 = bf16[128,3,1152]{2,0,1:T(8,128)(2,1)S(1)} all-gather(bf16[16,3,1152]{2,0,1:T(8,128)(2,1)S(1)} %copy.34), channel_id=1, replica_groups=mesh['sect'=4,'blk_0'=4,'blk_1'=4,'blk_2'=8] {'blk_2'}, dimensions={0}, use_global_device_ids=true | all-gather | bytes 995328 | tf_op jit(solution)/shard_map/all_gather | solution.py:28
  320.3 1.9 copy.35
  322.2 1.5 reshape_reshape.4
  325.1 1.5 convolution_reduce_fusion
  329.5 1.8 reshape.145
  331.4 26.4 %reduce-scatter.4.cloned.1.call-done = f32[32,3,1152]{2,0,1:T(8,128)} async-done(((f32[128,3,1152]{2,0,1:T(8,128)}), f32[32,3,1152]{2,0,1:T(8,128)}) %reduce-scatter.4.cloned.1.call-update) | async-done | bytes 442384 | tf_op jit(solution)/shard_map/reduce_scatter | solution.py:44
  358.7 16.7 %all-gather.2 = bf16[4,1076,9]{1,2,0:T(8,128)(2,1)S(1)} all-gather(bf16[1,1076,9]{1,2,0:T(8,128)(2,1)S(1)} %dynamic-slice_bitcast_fusion), channel_id=2, replica_groups=mesh['sect'=4,'blk_0'=4,'blk_1'=4,'blk_2'=8] {'blk_0'}, dimensions={0}, use_global_device_ids=true | all-gather | bytes 96840 | tf_op jit(solution)/shard_map/all_gather | solution.py:28
  375.4 13.0 %all_gather.31 = bf16[16,1076,9]{1,2,0:T(8,128)(2,1)S(1)} all-gather(bf16[4,1076,9]{1,2,0:T(8,128)(2,1)S(1)} %all-gather.2), channel_id=1, replica_groups=mesh['sect'=4,'blk_0'=4,'blk_1'=4,'blk_2'=8] {'blk_1'}, dimensions={0}, use_global_device_ids=true | all-gather | bytes 387360 | tf_op jit(solution)/shard_map/all_gather | solution.py:28
  392.4 47.4 %all-reduce.4.cloned.1.call-done = f32[32,3,1152]{2,0,1:T(8,128)} async-done(((f32[32,3,1152]{2,0,1:T(8,128)}), f32[32,3,1152]{2,0,1:T(8,128)}) %all-reduce.4.cloned.1.call-update) | async-done | bytes 442384
  440.8 21.6 %all-reduce.1 = f32[4,3,1152]{2,0,1:T(4,128)S(1)} all-reduce(f32[4,3,1152]{2,0,1:T(4,128)S(1)} %constant_dynamic-slice_fusion.1), channel_id=5, replica_groups=mesh['sect'=4,'blk_0'=4,'blk_1'=4,'blk_2'=8] {'blk_0'}, use_global_device_ids=true, to_apply=%region_6.7.clone | all-reduce | flops 13824 | bytes 110592
  463.6 3.3 all-to-all-start
  466.9 18.4 %all-gather.6.cloned.1.call-done = bf16[128,1076,9]{1,0,2:T(8,128)(2,1)} async-done(((bf16[16,1076,9]{1,0,2:T(8,128)(2,1)}), bf16[128,1076,9]{1,0,2:T(8,128)(2,1)}) %all-gather.6.cloned.1.call-update) | async-done | bytes 2479120 | tf_op jit(solution)/shard_map/all_gather | solution.py:28
  485.3 5.6 %reshape.146 = bf16[8,4,4,1076,9]{3,2,1,0,4:T(4,128)(2,1)} reshape(bf16[128,1076,9]{1,0,2:T(8,128)(2,1)} %all-gather.6.cloned.1.call-done) | data formatting | bytes 4958208 | tf_op jit(solution)/shard_map/reshape | solution.py:30
  490.9 5.6 %copy.41 = bf16[4,4,8,1076,9]{3,4,2,1,0:T(8,128)(2,1)} copy(bf16[4,4,8,1076,9]{3,0,1,2,4:T(4,128)(2,1)} %bitcast.69) | data formatting | bytes 4958208 | tf_op jit(solution)/shard_map/transpose | solution.py:22
  496.5 5.9 %reshape.148 = bf16[1076,1152]{0,1:T(8,128)(2,1)} reshape(bf16[1076,128,9]{0,2,1:T(8,128)(2,1)} %bitcast.68) | data formatting | bytes 4958208 | tf_op jit(solution)/shard_map/reshape | solution.py:22
  502.6 2.9 fusion.7
  (39 shorter events, 11.6 us)
Async XLA Ops:
  6.5 247.6 %copy-start = (bf16[1,192,4304]{2,1,0:T(8,128)(2,1)S(1)}, bf16[1,192,4304]{2,1,0:T(8,128)(2,1)}, u32[]{:S(2)}) copy-start(bf16[1,192,4304]{2,1,0:T(8,128)(2,1)} %param.8) | copy-start | bytes 4958212
  6.5 229.7 %all-gather.8.cloned.1.call-start = ((), (), s32[]{:S(2)}) async-start(), calls=%async_computation.4 | async-start | bytes 17965056 | tf_op jit(solution)/shard_map/all_gather | solution.py:95
  8.3 349.5 %reduce-scatter.4.cloned.1.call-start = ((), (), s32[]{:S(2)}) async-start(), calls=%async_computation.2 | async-start | bytes 2211840 | tf_op jit(solution)/shard_map/reduce_scatter | solution.py:44
  254.1 7.3 %copy-start.2 = (f32[1152]{0:T(1024)S(1)}, f32[1152]{0:T(1024)}, u32[]{:S(2)}) copy-start(f32[1152]{0:T(1024)} %param.11) | copy-start | bytes 13828
  319.1 4.6 copy-start.1
  331.3 108.5 %all-reduce.4.cloned.1.call-start = ((), (), s32[]{:S(2)}) async-start(), calls=%async_computation.5 | async-start | bytes 884736
  357.8 127.5 %all-gather.6.cloned.1.call-start = ((), (), s32[]{:S(2)}) async-start(), calls=%async_computation.3 | async-start | bytes 2985984 | tf_op jit(solution)/shard_map/all_gather | solution.py:28
  463.6 38.8 %all-to-all-start = ((f32[4,3,1152]{2,1,0:T(4,128)}), f32[4,3,1152]{2,1,0:T(4,128)S(1)}, u32[]{:S(2)}, u32[]{:S(2)}) async-start(f32[4,3,1152]{2,1,0:T(4,128)} %broadcast_in_dim.29), calls=%async_computation.1 | async-start | bytes 147456 | tf_op jit(solution)/shard_map/all_to_all | solution.py:60
Sparse Core Ops, SparseCore 0:
  11.7 224.5 all-gather.7
  331.5 26.2 reduce-scatter.3
  360.1 79.7 all-reduce.3
  441.8 43.4 all-gather.5
where the time goes:
time: 513 us; the launch traced here: 512 us
  waiting for transfers between devices  318 us (62%)
  blocking collectives  109 us (21%)
  local copies, waits for them, and re-layouts  50.2 us (10%)
  between operations  15.9 us (3%)
  matrix products  11.7 us (2%)
    all_gather x1, waiting for transfers between devices, on_device(): lax.all_gather(w_local, BLK, axis=1, tiled=True)  225 us
    all_gather x5, blocking collectives, gather_in_order(): parts = lax.all_gather(parts, axes[k], axis=0, tiled=True)  81.9 us
    unnamed x5, waiting for transfers between devices  47.5 us
    reduce_scatter x1, waiting for transfers between devices, reduced_to_own(): parts = lax.psum_scatter(parts, axes[k], scatter_dimension=0, tiled=True)  26.4 us
    unnamed x13, local copies, waits for them, and re-layouts  22.7 us
    unnamed x1, blocking collectives  21.6 us
    all_gather x1, waiting for transfers between devices, gather_in_order(): parts = lax.all_gather(parts, axes[k], axis=0, tiled=True)  18.4 us
  transfers between devices with their start and end apart: 5, of which 4 were waited for; matrix products, arithmetic and copies ran while one was open for 5% of the time, Pallas kernels for 0%

commit v1 on v0

--- a/solution.py
+++ b/solution.py
@@ -3,6 +3,7 @@
 from jax import lax
 from jax.sharding import Mesh
 from jax.sharding import PartitionSpec as P
+from jax.lax import all_to_all, axis_size
 
 D = 1152
 FF = 4304
@@ -79,6 +80,13 @@
     match_score_offset,
     caption_match_position,
 ):
+
+    def touch_the_shapes(array_axis, row_data):
+        return jnp.concatenate(
+            all_to_all(jnp.stack([row_data for _ in range(axis_size(BLK))]), BLK, 0, 0),
+            axis=array_axis,
+        )
+
     hidden = last_perceptron_activations[0]
     sect_index = lax.axis_index("sect")
     blk_index = lax.axis_index(BLK)
@@ -91,9 +99,7 @@
     is_text = sect_index == 0
     live = jnp.where(is_text, 0.0, 1.0).astype(jnp.float32)
     w_local = jnp.where(is_text, caption_reduction_matrix, picture_reduction_matrix)
-    outs = jnp.dot(
-        hidden, lax.all_gather(w_local, BLK, axis=1, tiled=True), preferred_element_type=jnp.float32
-    )
+    outs = jnp.dot(hidden, touch_the_shapes(1, w_local), preferred_element_type=jnp.float32)
     text_pool = jnp.mean(outs.reshape(txt_count, TXT_LEN, D), axis=1) + caption_offset_vector
     image_pool = jnp.mean(outs.reshape(img_count, IMG_TOK, D), axis=1) + picture_offset_vector
     text_pool = broadcast(text_pool, "sect", 0)

time: 513 us -> 908 us (1.77)
  waiting for transfers between devices: 318 us -> 615 us
  blocking collectives: 109 us -> 180 us
  starting transfers between devices: 3.41 us -> 23.9 us
    all_to_all x0 -> x1, waiting for transfers between devices: none -> 519 us  [touch_the_shapes(): all_to_all(jnp.stack([row_data for _ in range(axis_size(BLK))]), BLK, 0, 0)]
    all_gather x1 -> x0, waiting for transfers between devices: 225 us -> none  [on_device(): lax.all_gather(w_local, BLK, axis=1, tiled=True)]
    all_gather x5, blocking collectives: 81.9 us -> 153 us  [gather_in_order(): parts = lax.all_gather(parts, axes[k], axis=0, tiled=True)]
    all_to_all x0 -> x1, starting transfers between devices: none -> 20.3 us  [touch_the_shapes(): all_to_all(jnp.stack([row_data for _ in range(axis_size(BLK))]), BLK, 0, 0)]
    reshape x0 -> x1, local copies, waits for them, and re-layouts: none -> 17.9 us  [touch_the_shapes(): jnp.concatenate(all_to_all(jnp.stack([row_data for _ in range(axis_size(B...]
    unnamed x13 -> x12, local copies, waits for them, and re-layouts: 22.7 us -> 4.85 us
    unnamed x5 -> x4, waiting for transfers between devices: 47.5 us -> 47.5 us
  transfers between devices with their start and end apart: 5 -> 5, of which waited for: 4 -> 4; matrix products, arithmetic and copies ran while one was open for 5% -> 3% of each run, Pallas kernels for 0% -> 0%
where the time goes in v1:
time: 908 us; the launch traced here: 907 us
  waiting for transfers between devices  615 us (68%)
  blocking collectives  180 us (20%)
  local copies, waits for them, and re-layouts  56.5 us (6%)
  starting transfers between devices  23.9 us (3%)
  between operations  15.9 us (2%)
  matrix products  11.7 us (1%)
    all_to_all x1, waiting for transfers between devices, touch_the_shapes(): all_to_all(jnp.stack([row_data for _ in range(axis_size(BLK))]), BLK, 0, 0)  519 us
    all_gather x5, blocking collectives, gather_in_order(): parts = lax.all_gather(parts, axes[k], axis=0, tiled=True)  153 us
    unnamed x4, waiting for transfers between devices  47.5 us
    reduce_scatter x1, waiting for transfers between devices, reduced_to_own(): parts = lax.psum_scatter(parts, axes[k], scatter_dimension=0, tiled=True)  31 us
    unnamed x1, blocking collectives  21.6 us
    all_to_all x1, starting transfers between devices, touch_the_shapes(): all_to_all(jnp.stack([row_data for _ in range(axis_size(BLK))]), BLK, 0, 0)  20.3 us
    all_gather x1, waiting for transfers between devices, gather_in_order(): parts = lax.all_gather(parts, axes[k], axis=0, tiled=True)  18.4 us
  transfers between devices with their start and end apart: 5, of which 4 were waited for; matrix products, arithmetic and copies ran while one was open for 3% of the time, Pallas kernels for 0%

profile of v1, /device:TPU:2, one launch (start us, length us, event | category | flops | bytes accessed | tf_op | source)
XLA Modules:
  0.0 907.0 jit_solution(3853355753770131349)
XLA Ops:
  7.6 6.4 stack.2
  14.0 20.3 %all-to-all-start = ((bf16[128,4304,9]{1,2,0:T(8,128)(2,1)}), bf16[128,4304,9]{1,2,0:T(8,128)(2,1)}, u32[]{:S(2)}, u32[]{:S(2)}) async-start(bf16[128,4304,9]{1,2,0:T(8,128)(2,1)} %stack.2), calls=%async_computation | async-start | bytes 35651584 | tf_op jit(solution)/shard_map/all_to_all | solution.py:86
  36.9 518.5 %all-to-all-done = bf16[128,4304,9]{1,2,0:T(8,128)(2,1)} async-done(((bf16[128,4304,9]{1,2,0:T(8,128)(2,1)}), bf16[128,4304,9]{1,2,0:T(8,128)(2,1)}, u32[]{:S(2)}, u32[]{:S(2)}) %all-to-all-start) | async-done | bytes 9916448 | tf_op jit(solution)/shard_map/all_to_all | solution.py:86
  555.4 17.9 %reshape.151 = bf16[4304,1152]{0,1:T(8,128)(2,1)} reshape(bf16[4304,128,9]{0,2,1:T(8,128)(2,1)} %bitcast.2) | data formatting | bytes 19832832 | tf_op jit(solution)/shard_map/reshape | solution.py:85
  573.3 7.3 fusion.14
  580.6 5.3 all_gather.22
  586.1 44.0 %all_gather.23 = bf16[4,3,1152]{2,1,0:T(4,128)(2,1)S(1)} all-gather(bf16[1,3,1152]{2,1,0:T(4,128)(2,1)S(1)} %multiply_convert_fusion), channel_id=1, replica_groups=mesh['sect'=4,'blk_0'=4,'blk_1'=4,'blk_2'=8] {'blk_0'}, dimensions={0}, use_global_device_ids=true | all-gather | bytes 34560 | tf_op jit(solution)/shard_map/all_gather | solution.py:29
  630.1 10.8 %all_gather.24 = bf16[16,3,1152]{2,1,0:T(4,128)(2,1)S(1)} all-gather(bf16[4,3,1152]{2,1,0:T(4,128)(2,1)S(1)} %all_gather.23), channel_id=1, replica_groups=mesh['sect'=4,'blk_0'=4,'blk_1'=4,'blk_2'=8] {'blk_1'}, dimensions={0}, use_global_device_ids=true | all-gather | bytes 138240 | tf_op jit(solution)/shard_map/all_gather | solution.py:29
  640.9 68.5 %all_gather.25 = bf16[128,3,1152]{2,0,1:T(8,128)(2,1)S(1)} all-gather(bf16[16,3,1152]{2,0,1:T(8,128)(2,1)S(1)} %copy.35), channel_id=1, replica_groups=mesh['sect'=4,'blk_0'=4,'blk_1'=4,'blk_2'=8] {'blk_2'}, dimensions={0}, use_global_device_ids=true | all-gather | bytes 995328 | tf_op jit(solution)/shard_map/all_gather | solution.py:29
  710.5 1.9 copy.36
  712.5 1.5 reshape_reshape.4
  715.3 1.5 convolution_reduce_fusion
  719.7 1.8 reshape.155
  721.6 31.0 %reduce-scatter.4.cloned.1.call-done = f32[32,3,1152]{2,0,1:T(8,128)} async-done(((f32[128,3,1152]{2,0,1:T(8,128)}), f32[32,3,1152]{2,0,1:T(8,128)}) %reduce-scatter.4.cloned.1.call-update) | async-done | bytes 442384 | tf_op jit(solution)/shard_map/reduce_scatter | solution.py:45
  753.5 16.7 %all-gather.1 = bf16[4,1076,9]{1,2,0:T(8,128)(2,1)S(1)} all-gather(bf16[1,1076,9]{1,2,0:T(8,128)(2,1)S(1)} %dynamic-slice_bitcast_fusion), channel_id=2, replica_groups=mesh['sect'=4,'blk_0'=4,'blk_1'=4,'blk_2'=8] {'blk_0'}, dimensions={0}, use_global_device_ids=true | all-gather | bytes 96840 | tf_op jit(solution)/shard_map/all_gather | solution.py:29
  770.2 13.0 %all_gather.27 = bf16[16,1076,9]{1,2,0:T(8,128)(2,1)S(1)} all-gather(bf16[4,1076,9]{1,2,0:T(8,128)(2,1)S(1)} %all-gather.1), channel_id=1, replica_groups=mesh['sect'=4,'blk_0'=4,'blk_1'=4,'blk_2'=8] {'blk_1'}, dimensions={0}, use_global_device_ids=true | all-gather | bytes 387360 | tf_op jit(solution)/shard_map/all_gather | solution.py:29
  787.2 47.4 %all-reduce.4.cloned.1.call-done = f32[32,3,1152]{2,0,1:T(8,128)} async-done(((f32[32,3,1152]{2,0,1:T(8,128)}), f32[32,3,1152]{2,0,1:T(8,128)}) %all-reduce.4.cloned.1.call-update) | async-done | bytes 442384
  835.6 21.6 %all-reduce.1 = f32[4,3,1152]{2,0,1:T(4,128)S(1)} all-reduce(f32[4,3,1152]{2,0,1:T(4,128)S(1)} %constant_dynamic-slice_fusion.1), channel_id=5, replica_groups=mesh['sect'=4,'blk_0'=4,'blk_1'=4,'blk_2'=8] {'blk_0'}, use_global_device_ids=true, to_apply=%region_6.7.clone | all-reduce | flops 13824 | bytes 110592
  858.4 3.5 all-to-all-start.1
  861.8 18.4 %all-gather.4.cloned.1.call-done = bf16[128,1076,9]{1,0,2:T(8,128)(2,1)} async-done(((bf16[16,1076,9]{1,0,2:T(8,128)(2,1)}), bf16[128,1076,9]{1,0,2:T(8,128)(2,1)}) %all-gather.4.cloned.1.call-update) | async-done | bytes 2479120 | tf_op jit(solution)/shard_map/all_gather | solution.py:29
  880.2 5.6 reshape.156
  885.8 5.6 copy.42
  891.4 5.9 reshape.158
  897.6 2.9 fusion.7
  (39 shorter events, 13.9 us)
Async XLA Ops:
  6.5 566.8 %copy-start = (bf16[1,192,4304]{2,1,0:T(8,128)(2,1)S(1)}, bf16[1,192,4304]{2,1,0:T(8,128)(2,1)}, u32[]{:S(2)}) copy-start(bf16[1,192,4304]{2,1,0:T(8,128)(2,1)} %param.8) | copy-start | bytes 4958212
  14.0 541.5 %all-to-all-start = ((bf16[128,4304,9]{1,2,0:T(8,128)(2,1)}), bf16[128,4304,9]{1,2,0:T(8,128)(2,1)}, u32[]{:S(2)}, u32[]{:S(2)}) async-start(bf16[128,4304,9]{1,2,0:T(8,128)(2,1)} %stack.2), calls=%async_computation | async-start | bytes 35651584 | tf_op jit(solution)/shard_map/all_to_all | solution.py:86
  34.3 718.3 %reduce-scatter.4.cloned.1.call-start = ((), (), s32[]{:S(2)}) async-start(), calls=%async_computation.3 | async-start | bytes 2211840 | tf_op jit(solution)/shard_map/reduce_scatter | solution.py:45
  573.3 7.3 copy-start.2
  709.4 4.6 copy-start.1
  721.6 113.1 %all-reduce.4.cloned.1.call-start = ((), (), s32[]{:S(2)}) async-start(), calls=%async_computation.5 | async-start | bytes 884736
  752.6 127.6 %all-gather.4.cloned.1.call-start = ((), (), s32[]{:S(2)}) async-start(), calls=%async_computation.4 | async-start | bytes 2985984 | tf_op jit(solution)/shard_map/all_gather | solution.py:29
  858.4 39.0 %all-to-all-start.1 = ((f32[4,3,1152]{2,1,0:T(4,128)}), f32[4,3,1152]{2,1,0:T(4,128)S(1)}, u32[]{:S(2)}, u32[]{:S(2)}) async-start(f32[4,3,1152]{2,1,0:T(4,128)} %broadcast_in_dim.29), calls=%async_computation.2 | async-start | bytes 147456 | tf_op jit(solution)/shard_map/all_to_all | solution.py:61
Sparse Core Ops, SparseCore 0:
  721.7 30.8 reduce-scatter.3
  754.9 79.7 all-reduce.3
  836.7 43.4 all-gather.3
